TPU v7x, 512 devices: a whole 4x4x16 slice. The times are simulated.
512 devices in a mesh: dp: 8 (over y, core), expert: 64 (over x, z).
Axes of the slice: x: 4, y: 4, z: 16, core: 2. Of those that a mesh axis runs over, the one named last changes fastest.
Arguments:
- tokens: bfloat16 [65536, 4096], P(('dp', 'expert')), may hold values from -6 to 6
- expert_ids: int32 [65536, 2], P(('dp', 'expert')), may hold values from 0 to 63, as said below
- gate_values: float32 [65536, 2], P(('dp', 'expert')), may hold values from 0.2 to 1
- w_gate: bfloat16 [4096, 14336], P('dp', 'expert'), may hold values from -0.09375 to 0.09375
- w_up: bfloat16 [4096, 14336], P('dp', 'expert'), may hold values from -0.09375 to 0.09375
- w_down: bfloat16 [14336, 4096], P('expert', 'dp'), may hold values from -0.046875 to 0.046875
- target: bfloat16 [65536, 4096], P(('dp', 'expert')), may hold values from -6 to 6
Outputs:
- token_grad: bfloat16 [65536, 4096], P(('dp', 'expert'))
- gate_grad: bfloat16 [4096, 14336], P('dp', 'expert')
- up_grad: bfloat16 [4096, 14336], P('dp', 'expert')
Inputs may be any that keep to these rules, and one draw needn't show every extreme that they name: `expert_ids`: A token's two expert ids differ, and no token names two experts below 1. Among the 128 tokens of one device each expert below 1 is named by 1 to 3 tokens, and in every draw some device names each of them exactly 3 times.
All inputs are finite; a program needn't handle non-finite values.
Results may differ from a plain program's by a relative error of at most 0.008.
Values may be sent and summed in bfloat16 or wider, within the bound.
A program may use at most 64 MiB of HBM per device.

v0:
```python
import jax
import jax.numpy as jnp
from jax import lax
from jax.sharding import PartitionSpec as P

EXPERTS = 1


def contract_last(matrix_a, matrix_b):
    return lax.dot_general(
        matrix_a, matrix_b, (((1,), (1,)), ((), ())), preferred_element_type=jnp.float32
    )


def rounded_terms(column_blocks, grad_blocks):
    terms = jnp.einsum(
        "krd,krh->kdh", column_blocks, grad_blocks, preferred_element_type=jnp.float32
    )
    terms = lax.optimization_barrier(terms.astype(jnp.bfloat16))
    return jnp.sum(terms.astype(jnp.float32), axis=0)


def spread_rows(rows, group_size, capacity, features):
    flat = rows.reshape(EXPERTS, 1, capacity * features)
    wide = jnp.broadcast_to(flat, (EXPERTS, group_size, capacity * features))
    return wide.reshape(EXPERTS * group_size * capacity, features)


def fold_group(rows, group_size, capacity, features):
    shaped = rows.reshape(EXPERTS, group_size, capacity * features).astype(jnp.float32)
    return jnp.sum(shaped, axis=1).reshape(EXPERTS * capacity, features)


def shards(tokens, expert_ids, gate_values, w_gate, w_up, w_down, target):
    devices_along = lax.axis_size("expert")
    group_size = devices_along // EXPERTS
    tok_rows = tokens.shape[0]
    features = tokens.shape[1]
    hid_local = w_gate.shape[1]
    capacity = max(2, 3 * tok_rows // 128)
    slot_total = EXPERTS * capacity
    flat_ids = expert_ids.reshape(-1)
    pair_count = flat_ids.shape[0]
    window = flat_ids < EXPERTS
    onehot = (flat_ids[:, None] == jnp.arange(EXPERTS, dtype=jnp.int32)[None, :]).astype(jnp.int32)
    slot_index = jnp.sum((jnp.cumsum(onehot, axis=0) - onehot) * onehot, axis=1)
    position = jnp.where(window, flat_ids * capacity + slot_index, slot_total)
    owning = jnp.arange(pair_count, dtype=jnp.int32) // 2
    slot_token = jnp.zeros((slot_total + 1,), jnp.int32).at[position].set(owning)[:slot_total]
    slot_live = jnp.zeros((slot_total + 1,), jnp.bool_).at[position].set(True)[:slot_total]
    slot_gate = (
        jnp.zeros((slot_total + 1,), jnp.float32)
        .at[position]
        .set(gate_values.reshape(-1))[:slot_total]
    )
    safe_pairs = jnp.minimum(position, slot_total - 1).reshape(tok_rows, 2)
    live_pairs = window.reshape(tok_rows, 2)

    def pick(table, column):
        return jnp.where(live_pairs[:, column : column + 1], table[safe_pairs[:, column]], 0.0)

    outgoing = jnp.where(slot_live[:, None], tokens[slot_token], jnp.zeros((), tokens.dtype))
    outgoing = spread_rows(outgoing, group_size, capacity, features)
    received = lax.all_to_all(outgoing, "expert", split_axis=0, concat_axis=0, tiled=True)
    rows_count = received.shape[0]
    full_gate, full_up, full_down = (
        lax.all_gather(w_gate, "dp", axis=0, tiled=True),
        lax.all_gather(w_up, "dp", axis=0, tiled=True),
        lax.all_gather(w_down, "dp", axis=1, tiled=True),
    )
    gate_pre = jnp.dot(received, full_gate, preferred_element_type=jnp.float32)
    up_pre = jnp.dot(received, full_up, preferred_element_type=jnp.float32)
    sigmoid_gate = jax.nn.sigmoid(gate_pre)
    activated = sigmoid_gate * gate_pre
    hidden = (activated * up_pre).astype(jnp.bfloat16)
    partial_out = jnp.dot(hidden, full_down, preferred_element_type=jnp.float32).astype(
        jnp.bfloat16
    )
    returned_out = lax.all_to_all(partial_out, "expert", split_axis=0, concat_axis=0, tiled=True)
    expert_out = fold_group(returned_out, group_size, capacity, features)
    combined = gate_values[:, 0:1] * pick(expert_out, 0) + gate_values[:, 1:2] * pick(expert_out, 1)
    residual = combined - target.astype(jnp.float32)
    outgoing_grad = jnp.where(
        slot_live[:, None], slot_gate[:, None] * residual[slot_token], 0.0
    ).astype(jnp.bfloat16)
    outgoing_grad = spread_rows(outgoing_grad, group_size, capacity, features)
    cotangent = lax.all_to_all(outgoing_grad, "expert", split_axis=0, concat_axis=0, tiled=True)
    grad_hidden = contract_last(cotangent, full_down)
    derivative = sigmoid_gate * (1.0 + gate_pre * (1.0 - sigmoid_gate))
    grad_gate_pre = (grad_hidden * up_pre * derivative).astype(jnp.bfloat16)
    grad_up_pre = (grad_hidden * activated).astype(jnp.bfloat16)
    row_part = (
        contract_last(grad_gate_pre, full_gate) + contract_last(grad_up_pre, full_up)
    ).astype(jnp.bfloat16)
    back_rows = lax.all_to_all(row_part, "expert", split_axis=0, concat_axis=0, tiled=True)
    row_grad = fold_group(back_rows, group_size, capacity, features)
    token_grad = (pick(row_grad, 0) + pick(row_grad, 1)).astype(jnp.bfloat16)
    shard_columns = lax.all_to_all(received, "dp", split_axis=1, concat_axis=0, tiled=True)
    shard_width = shard_columns.shape[1]
    dp_count = lax.axis_size("dp")
    every_gate, every_up = (
        lax.all_gather(grad_gate_pre, "dp", axis=0, tiled=True),
        lax.all_gather(grad_up_pre, "dp", axis=0, tiled=True),
    )
    column_blocks = shard_columns.reshape(dp_count, rows_count, shard_width)
    gate_sum = rounded_terms(column_blocks, every_gate.reshape(dp_count, rows_count, hid_local))
    up_sum = rounded_terms(column_blocks, every_up.reshape(dp_count, rows_count, hid_local))
    return (token_grad, gate_sum.astype(jnp.bfloat16), up_sum.astype(jnp.bfloat16))


def solution(mesh):
    placed = (
        P(("dp", "expert"), None),
        P(("dp", "expert"), None),
        P(("dp", "expert"), None),
        P("dp", "expert"),
        P("dp", "expert"),
        P("expert", "dp"),
        P(("dp", "expert"), None),
    )
    return jax.shard_map(
        shards,
        mesh=mesh,
        in_specs=placed,
        out_specs=(P(("dp", "expert"), None), P("dp", "expert"), P("dp", "expert")),
        check_vma=False,
    )
```

profile of v0, /device:TPU:6, one launch (start us, length us, event | category | flops | bytes accessed | tf_op | source)
XLA Modules:
  0.0 524.1 jit_solution(15885397472876217078)
XLA Ops:
  16.4 18.8 %all-to-all-start = ((bf16[64,3,4096]{2,1,0:T(4,128)(2,1)}), bf16[64,3,4096]{2,1,0:T(4,128)(2,1)S(1)}, u32[]{:S(2)}, u32[]{:S(2)}) async-start(bf16[64,3,4096]{2,1,0:T(4,128)(2,1)} %broadcast_in_dim.87), calls=%async_computation | async-start | bytes 4194304 | tf_op jit(solution)/shard_map/all_to_all | solution.py:64
  36.7 95.8 %all-to-all-done = bf16[64,3,4096]{2,1,0:T(4,128)(2,1)S(1)} async-done(((bf16[64,3,4096]{2,1,0:T(4,128)(2,1)}), bf16[64,3,4096]{2,1,0:T(4,128)(2,1)S(1)}, u32[]{:S(2)}, u32[]{:S(2)}) %all-to-all-start) | async-done | bytes 1572896 | tf_op jit(solution)/shard_map/all_to_all | solution.py:64
  135.0 2.7 fusion.16
  137.8 3.4 fusion.15
  141.2 3.4 convolution_convert_fusion
  144.5 4.1 all_to_all.38
  148.6 8.6 %all-to-all-start.1 = ((bf16[64,3,4096]{2,1,0:T(4,128)(2,1)}), bf16[64,3,4096]{2,1,0:T(4,128)(2,1)}, u32[]{:S(2)}, u32[]{:S(2)}) async-start(bf16[64,3,4096]{2,1,0:T(4,128)(2,1)} %all_to_all.38), calls=%async_computation.1 | async-start | bytes 4194304 | tf_op jit(solution)/shard_map/all_to_all | solution.py:79
  159.5 94.7 %all-to-all-done.1 = bf16[64,3,4096]{2,1,0:T(4,128)(2,1)} async-done(((bf16[64,3,4096]{2,1,0:T(4,128)(2,1)}), bf16[64,3,4096]{2,1,0:T(4,128)(2,1)}, u32[]{:S(2)}, u32[]{:S(2)}) %all-to-all-start.1) | async-done | bytes 1572896 | tf_op jit(solution)/shard_map/all_to_all | solution.py:79
  261.3 4.6 convert_subtract_fusion
  270.5 8.8 %all-to-all-start.2 = ((bf16[64,3,4096]{2,1,0:T(4,128)(2,1)}), bf16[64,3,4096]{2,1,0:T(4,128)(2,1)}, u32[]{:S(2)}, u32[]{:S(2)}) async-start(bf16[64,3,4096]{2,1,0:T(4,128)(2,1)} %broadcast_in_dim.92), calls=%async_computation.2 | async-start | bytes 4194304 | tf_op jit(solution)/shard_map/all_to_all | solution.py:87
  279.3 3.1 all_to_all.44
  282.4 3.0 copy.20
  285.4 90.8 %all-to-all-done.2 = bf16[64,3,4096]{2,1,0:T(4,128)(2,1)} async-done(((bf16[64,3,4096]{2,1,0:T(4,128)(2,1)}), bf16[64,3,4096]{2,1,0:T(4,128)(2,1)}, u32[]{:S(2)}, u32[]{:S(2)}) %all-to-all-start.2) | async-done | bytes 1572896 | tf_op jit(solution)/shard_map/all_to_all | solution.py:87
  376.2 4.5 all-to-all-start.4
  380.7 4.3 all_to_all.41
  385.0 2.8 multiply_convert_fusion
  391.2 4.1 all_to_all.42
  395.2 7.0 %all-to-all-done.4 = bf16[192,8,512]{2,0,1:T(8,128)(2,1)S(1)} async-done(((bf16[192,8,512]{2,0,1:T(8,128)(2,1)}), bf16[192,8,512]{2,0,1:T(8,128)(2,1)S(1)}, u32[]{:S(2)}, u32[]{:S(2)}) %all-to-all-start.4) | async-done | bytes 1572896 | tf_op jit(solution)/shard_map/all_to_all | solution.py:98
  402.2 8.9 %all-to-all-start.3 = ((bf16[64,3,4096]{2,1,0:T(4,128)(2,1)}), bf16[64,3,4096]{2,1,0:T(4,128)(2,1)}, u32[]{:S(2)}, u32[]{:S(2)}) async-start(bf16[64,3,4096]{2,1,0:T(4,128)(2,1)} %all_to_all.42), calls=%async_computation.3 | async-start | bytes 4194304 | tf_op jit(solution)/shard_map/all_to_all | solution.py:95
  411.1 13.4 %all_gather.19 = bf16[1536,224]{1,0:T(8,128)(2,1)S(1)} all-gather(bf16[192,224]{1,0:T(8,128)(2,1)S(1)} %get-tuple-element.11), channel_id=1, replica_groups=mesh['dp'=8,'expert'=64] {'dp'}, dimensions={0}, use_global_device_ids=true | all-gather | bytes 774144 | tf_op jit(solution)/shard_map/all_gather | solution.py:103
  426.6 13.6 %all_gather.18 = bf16[1536,224]{1,0:T(8,128)(2,1)S(1)} all-gather(bf16[192,224]{1,0:T(8,128)(2,1)S(1)} %get-tuple-element.12), channel_id=1, replica_groups=mesh['dp'=8,'expert'=64] {'dp'}, dimensions={0}, use_global_device_ids=true | all-gather | bytes 774144 | tf_op jit(solution)/shard_map/all_gather | solution.py:102
  442.3 2.6 reduce_sum.49
  445.9 62.7 %all-to-all-done.3 = bf16[64,3,4096]{2,1,0:T(4,128)(2,1)} async-done(((bf16[64,3,4096]{2,1,0:T(4,128)(2,1)}), bf16[64,3,4096]{2,1,0:T(4,128)(2,1)}, u32[]{:S(2)}, u32[]{:S(2)}) %all-to-all-start.3) | async-done | bytes 1572896 | tf_op jit(solution)/shard_map/all_to_all | solution.py:95
  514.6 3.0 add_convert_fusion
  (67 shorter events, 41.4 us)
Async XLA Ops:
  7.2 6.2 %copy-start = (bf16[128,4096]{1,0:T(8,128)(2,1)S(1)}, bf16[128,4096]{1,0:T(8,128)(2,1)}, u32[]{:S(2)}) copy-start(bf16[128,4096]{1,0:T(8,128)(2,1)} %param.7) | copy-start | bytes 3145732
  7.2 127.9 %all-gather.6.cloned.1.call-start = ((), (), s32[]{:S(2)}) async-start(), calls=%async_computation.6 | async-start | bytes 2064384 | tf_op jit(solution)/shard_map/all_gather | solution.py:68
  16.4 116.1 %all-to-all-start = ((bf16[64,3,4096]{2,1,0:T(4,128)(2,1)}), bf16[64,3,4096]{2,1,0:T(4,128)(2,1)S(1)}, u32[]{:S(2)}, u32[]{:S(2)}) async-start(bf16[64,3,4096]{2,1,0:T(4,128)(2,1)} %broadcast_in_dim.87), calls=%async_computation | async-start | bytes 4194304 | tf_op jit(solution)/shard_map/all_to_all | solution.py:64
  35.2 102.6 %all-gather.4.cloned.1.call-start = ((), (), s32[]{:S(2)}) async-start(), calls=%async_computation.5 | async-start | bytes 2064384 | tf_op jit(solution)/shard_map/all_gather | solution.py:67
  35.9 105.2 %all-gather.8.cloned.1.call-start = ((), (), s32[]{:S(2)}) async-start(), calls=%async_computation.7 | async-start | bytes 2064384 | tf_op jit(solution)/shard_map/all_gather | solution.py:69
  148.6 8.6 %copy-start.5 = (f32[128,2]{0,1:T(2,128)S(1)}, f32[128,2]{0,1:T(2,128)}, u32[]{:S(2)}) copy-start(f32[128,2]{0,1:T(2,128)} %param.9) | copy-start | bytes 3076
  148.6 105.6 %all-to-all-start.1 = ((bf16[64,3,4096]{2,1,0:T(4,128)(2,1)}), bf16[64,3,4096]{2,1,0:T(4,128)(2,1)}, u32[]{:S(2)}, u32[]{:S(2)}) async-start(bf16[64,3,4096]{2,1,0:T(4,128)(2,1)} %all_to_all.38), calls=%async_computation.1 | async-start | bytes 4194304 | tf_op jit(solution)/shard_map/all_to_all | solution.py:79
  270.5 105.7 %all-to-all-start.2 = ((bf16[64,3,4096]{2,1,0:T(4,128)(2,1)}), bf16[64,3,4096]{2,1,0:T(4,128)(2,1)}, u32[]{:S(2)}, u32[]{:S(2)}) async-start(bf16[64,3,4096]{2,1,0:T(4,128)(2,1)} %broadcast_in_dim.92), calls=%async_computation.2 | async-start | bytes 4194304 | tf_op jit(solution)/shard_map/all_to_all | solution.py:87
  376.2 26.0 %all-to-all-start.4 = ((bf16[192,8,512]{2,0,1:T(8,128)(2,1)}), bf16[192,8,512]{2,0,1:T(8,128)(2,1)S(1)}, u32[]{:S(2)}, u32[]{:S(2)}) async-start(bf16[192,8,512]{2,0,1:T(8,128)(2,1)} %copy.20), calls=%async_computation.4 | async-start | bytes 3145728 | tf_op jit(solution)/shard_map/all_to_all | solution.py:98
  380.7 4.3 copy-start.4
  385.0 2.8 copy-start.2
  387.9 1.5 copy-start.1
  402.2 106.4 %all-to-all-start.3 = ((bf16[64,3,4096]{2,1,0:T(4,128)(2,1)}), bf16[64,3,4096]{2,1,0:T(4,128)(2,1)}, u32[]{:S(2)}, u32[]{:S(2)}) async-start(bf16[64,3,4096]{2,1,0:T(4,128)(2,1)} %all_to_all.42), calls=%async_computation.3 | async-start | bytes 4194304 | tf_op jit(solution)/shard_map/all_to_all | solution.py:95
  442.3 2.6 copy-start.3
Sparse Core Ops, SparseCore 0:
  10.1 36.9 all-gather.5
  49.2 32.8 all-gather.3
  84.3 32.8 all-gather.7
where the time goes:
time: 525 us; the launch traced here: 524 us
  waiting for transfers between devices  353 us (67%)
  starting transfers between devices  49.6 us (9%)
  local copies, waits for them, and re-layouts  44.5 us (8%)
  blocking collectives  27 us (5%)
  matrix products  18.8 us (4%)
  other arithmetic  17 us (3%)
  between operations  14 us (3%)
    all_to_all x1, waiting for transfers between devices, shards(): lax.all_to_all(outgoing, 'expert', split_axis=0, concat_axis=0, tiled=True)  95.8 us
    all_to_all x1, waiting for transfers between devices, shards(): lax.all_to_all(partial_out, 'expert', split_axis=0, concat_axis=0, tiled=...  94.7 us
    all_to_all x1, waiting for transfers between devices, shards(): lax.all_to_all(outgoing_grad, 'expert', split_axis=0, concat_axis=0, tile...  90.8 us
    all_to_all x1, waiting for transfers between devices, shards(): lax.all_to_all(row_part, 'expert', split_axis=0, concat_axis=0, tiled=True)  62.7 us
    all_to_all x1, starting transfers between devices, shards(): lax.all_to_all(outgoing, 'expert', split_axis=0, concat_axis=0, tiled=True)  18.8 us
    all_gather x1, blocking collectives, shards(): lax.all_gather(grad_gate_pre, 'dp', axis=0, tiled=True)  13.6 us
    all_gather x1, blocking collectives, shards(): lax.all_gather(grad_up_pre, 'dp', axis=0, tiled=True)  13.4 us
  transfers between devices with their start and end apart: 8, of which 5 were waited for; matrix products, arithmetic and copies ran while one was open for 6% of the time, Pallas kernels for 0%

commit v1 on v0

--- a/solution.py
+++ b/solution.py
@@ -99,7 +99,9 @@
     shard_width = shard_columns.shape[1]
     dp_count = lax.axis_size("dp")
     every_gate, every_up = (
-        lax.all_gather(grad_gate_pre, "dp", axis=0, tiled=True),
+        jnp.concatenate(
+            lax.all_to_all(jnp.stack([grad_gate_pre] * lax.axis_size("dp")), "dp", 0, 0), axis=0
+        ),
         lax.all_gather(grad_up_pre, "dp", axis=0, tiled=True),
     )
     column_blocks = shard_columns.reshape(dp_count, rows_count, shard_width)

time: 525 us -> 543 us (1.034)
  waiting for transfers between devices: 353 us -> 378 us
  blocking collectives: 27 us -> 13.6 us
    all_gather x1 -> x0, blocking collectives: 13.6 us -> none  [shards(): lax.all_gather(grad_gate_pre, 'dp', axis=0, tiled=True)]
    all_to_all x1, waiting for transfers between devices: 62.7 us -> 74.7 us  [shards(): lax.all_to_all(row_part, 'expert', split_axis=0, concat_axis=0, tiled=True)]
    all_to_all x1, waiting for transfers between devices: 7 us -> 14.5 us  [shards(): lax.all_to_all(received, 'dp', split_axis=1, concat_axis=0, tiled=True)]
  transfers between devices with their start and end apart: 8 -> 9, of which waited for: 5 -> 6; matrix products, arithmetic and copies ran while one was open for 6% -> 7% of each run, Pallas kernels for 0% -> 0%
where the time goes in v1:
time: 543 us; the launch traced here: 542 us
  waiting for transfers between devices  378 us (70%)
  starting transfers between devices  53.2 us (10%)
  local copies, waits for them, and re-layouts  44.6 us (8%)
  matrix products  20.4 us (4%)
  other arithmetic  18.4 us (3%)
  between operations  14 us (3%)
  blocking collectives  13.6 us (3%)
    all_to_all x1, waiting for transfers between devices, shards(): lax.all_to_all(outgoing, 'expert', split_axis=0, concat_axis=0, tiled=True)  95.8 us
    all_to_all x1, waiting for transfers between devices, shards(): lax.all_to_all(partial_out, 'expert', split_axis=0, concat_axis=0, tiled=...  94.7 us
    all_to_all x1, waiting for transfers between devices, shards(): lax.all_to_all(outgoing_grad, 'expert', split_axis=0, concat_axis=0, tile...  90.8 us
    all_to_all x1, waiting for transfers between devices, shards(): lax.all_to_all(row_part, 'expert', split_axis=0, concat_axis=0, tiled=True)  74.7 us
    all_to_all x1, starting transfers between devices, shards(): lax.all_to_all(outgoing, 'expert', split_axis=0, concat_axis=0, tiled=True)  18.8 us
    all_to_all x1, waiting for transfers between devices, shards(): lax.all_to_all(received, 'dp', split_axis=1, concat_axis=0, tiled=True)  14.5 us
    all_gather x1, blocking collectives, shards(): lax.all_gather(grad_up_pre, 'dp', axis=0, tiled=True)  13.6 us
  transfers between devices with their start and end apart: 9, of which 6 were waited for; matrix products, arithmetic and copies ran while one was open for 7% of the time, Pallas kernels for 0%

profile of v1, /device:TPU:6, one launch (start us, length us, event | category | flops | bytes accessed | tf_op | source)
XLA Modules:
  0.0 541.7 jit_solution(895550880512408620)
XLA Ops:
  16.4 18.8 %all-to-all-start = ((bf16[64,3,4096]{2,1,0:T(4,128)(2,1)}), bf16[64,3,4096]{2,1,0:T(4,128)(2,1)S(1)}, u32[]{:S(2)}, u32[]{:S(2)}) async-start(bf16[64,3,4096]{2,1,0:T(4,128)(2,1)} %broadcast_in_dim.87), calls=%async_computation | async-start | bytes 4194304 | tf_op jit(solution)/shard_map/all_to_all | solution.py:64
  36.7 95.8 %all-to-all-done = bf16[64,3,4096]{2,1,0:T(4,128)(2,1)S(1)} async-done(((bf16[64,3,4096]{2,1,0:T(4,128)(2,1)}), bf16[64,3,4096]{2,1,0:T(4,128)(2,1)S(1)}, u32[]{:S(2)}, u32[]{:S(2)}) %all-to-all-start) | async-done | bytes 1572896 | tf_op jit(solution)/shard_map/all_to_all | solution.py:64
  135.0 2.7 fusion.16
  137.8 3.4 fusion.15
  141.2 3.4 convolution_convert_fusion
  144.5 4.1 all_to_all.41
  148.6 8.6 %all-to-all-start.1 = ((bf16[64,3,4096]{2,1,0:T(4,128)(2,1)}), bf16[64,3,4096]{2,1,0:T(4,128)(2,1)}, u32[]{:S(2)}, u32[]{:S(2)}) async-start(bf16[64,3,4096]{2,1,0:T(4,128)(2,1)} %all_to_all.41), calls=%async_computation.1 | async-start | bytes 4194304 | tf_op jit(solution)/shard_map/all_to_all | solution.py:79
  159.5 94.7 %all-to-all-done.1 = bf16[64,3,4096]{2,1,0:T(4,128)(2,1)} async-done(((bf16[64,3,4096]{2,1,0:T(4,128)(2,1)}), bf16[64,3,4096]{2,1,0:T(4,128)(2,1)}, u32[]{:S(2)}, u32[]{:S(2)}) %all-to-all-start.1) | async-done | bytes 1572896 | tf_op jit(solution)/shard_map/all_to_all | solution.py:79
  261.3 4.6 convert_subtract_fusion
  270.5 8.8 %all-to-all-start.2 = ((bf16[64,3,4096]{2,1,0:T(4,128)(2,1)}), bf16[64,3,4096]{2,1,0:T(4,128)(2,1)}, u32[]{:S(2)}, u32[]{:S(2)}) async-start(bf16[64,3,4096]{2,1,0:T(4,128)(2,1)} %broadcast_in_dim.92), calls=%async_computation.2 | async-start | bytes 4194304 | tf_op jit(solution)/shard_map/all_to_all | solution.py:87
  279.3 3.1 all_to_all.47
  282.4 3.0 copy.20
  285.4 90.8 %all-to-all-done.2 = bf16[64,3,4096]{2,1,0:T(4,128)(2,1)} async-done(((bf16[64,3,4096]{2,1,0:T(4,128)(2,1)}), bf16[64,3,4096]{2,1,0:T(4,128)(2,1)}, u32[]{:S(2)}, u32[]{:S(2)}) %all-to-all-start.2) | async-done | bytes 1572896 | tf_op jit(solution)/shard_map/all_to_all | solution.py:87
  376.2 4.5 all-to-all-start.4
  380.7 4.3 all_to_all.44
  385.0 2.7 multiply_convert_fusion
  387.8 14.5 %all-to-all-done.4 = bf16[192,8,512]{2,0,1:T(8,128)(2,1)S(1)} async-done(((bf16[192,8,512]{2,0,1:T(8,128)(2,1)}), bf16[192,8,512]{2,0,1:T(8,128)(2,1)S(1)}, u32[]{:S(2)}, u32[]{:S(2)}) %all-to-all-start.4) | async-done | bytes 1572896 | tf_op jit(solution)/shard_map/all_to_all | solution.py:98
  403.2 3.5 all-to-all-start.5
  410.8 4.1 all_to_all.45
  414.9 4.9 all-to-all-done.5
  419.8 8.9 %all-to-all-start.3 = ((bf16[64,3,4096]{2,1,0:T(4,128)(2,1)}), bf16[64,3,4096]{2,1,0:T(4,128)(2,1)}, u32[]{:S(2)}, u32[]{:S(2)}) async-start(bf16[64,3,4096]{2,1,0:T(4,128)(2,1)} %all_to_all.45), calls=%async_computation.3 | async-start | bytes 4194304 | tf_op jit(solution)/shard_map/all_to_all | solution.py:95
  428.6 13.6 %all_gather.15 = bf16[1536,224]{1,0:T(8,128)(2,1)S(1)} all-gather(bf16[192,224]{1,0:T(8,128)(2,1)S(1)} %get-tuple-element.11), channel_id=1, replica_groups=mesh['dp'=8,'expert'=64] {'dp'}, dimensions={0}, use_global_device_ids=true | all-gather | bytes 774144 | tf_op jit(solution)/shard_map/all_gather | solution.py:105
  451.5 74.7 %all-to-all-done.3 = bf16[64,3,4096]{2,1,0:T(4,128)(2,1)} async-done(((bf16[64,3,4096]{2,1,0:T(4,128)(2,1)}), bf16[64,3,4096]{2,1,0:T(4,128)(2,1)}, u32[]{:S(2)}, u32[]{:S(2)}) %all-to-all-start.3) | async-done | bytes 1572896 | tf_op jit(solution)/shard_map/all_to_all | solution.py:95
  532.1 3.0 add_convert_fusion
  (67 shorter events, 47.1 us)
Async XLA Ops:
  7.2 6.2 %copy-start = (bf16[128,4096]{1,0:T(8,128)(2,1)S(1)}, bf16[128,4096]{1,0:T(8,128)(2,1)}, u32[]{:S(2)}) copy-start(bf16[128,4096]{1,0:T(8,128)(2,1)} %param.7) | copy-start | bytes 3145732
  7.2 127.9 %all-gather.6.cloned.1.call-start = ((), (), s32[]{:S(2)}) async-start(), calls=%async_computation.7 | async-start | bytes 2064384 | tf_op jit(solution)/shard_map/all_gather | solution.py:68
  16.4 116.1 %all-to-all-start = ((bf16[64,3,4096]{2,1,0:T(4,128)(2,1)}), bf16[64,3,4096]{2,1,0:T(4,128)(2,1)S(1)}, u32[]{:S(2)}, u32[]{:S(2)}) async-start(bf16[64,3,4096]{2,1,0:T(4,128)(2,1)} %broadcast_in_dim.87), calls=%async_computation | async-start | bytes 4194304 | tf_op jit(solution)/shard_map/all_to_all | solution.py:64
  35.2 102.6 %all-gather.4.cloned.1.call-start = ((), (), s32[]{:S(2)}) async-start(), calls=%async_computation.6 | async-start | bytes 2064384 | tf_op jit(solution)/shard_map/all_gather | solution.py:67
  35.9 105.2 %all-gather.8.cloned.1.call-start = ((), (), s32[]{:S(2)}) async-start(), calls=%async_computation.8 | async-start | bytes 2064384 | tf_op jit(solution)/shard_map/all_gather | solution.py:69
  148.6 8.6 %copy-start.4 = (f32[128,2]{0,1:T(2,128)S(1)}, f32[128,2]{0,1:T(2,128)}, u32[]{:S(2)}) copy-start(f32[128,2]{0,1:T(2,128)} %param.9) | copy-start | bytes 3076
  148.6 105.5 %all-to-all-start.1 = ((bf16[64,3,4096]{2,1,0:T(4,128)(2,1)}), bf16[64,3,4096]{2,1,0:T(4,128)(2,1)}, u32[]{:S(2)}, u32[]{:S(2)}) async-start(bf16[64,3,4096]{2,1,0:T(4,128)(2,1)} %all_to_all.41), calls=%async_computation.1 | async-start | bytes 4194304 | tf_op jit(solution)/shard_map/all_to_all | solution.py:79
  270.5 105.7 %all-to-all-start.2 = ((bf16[64,3,4096]{2,1,0:T(4,128)(2,1)}), bf16[64,3,4096]{2,1,0:T(4,128)(2,1)}, u32[]{:S(2)}, u32[]{:S(2)}) async-start(bf16[64,3,4096]{2,1,0:T(4,128)(2,1)} %broadcast_in_dim.92), calls=%async_computation.2 | async-start | bytes 4194304 | tf_op jit(solution)/shard_map/all_to_all | solution.py:87
  376.2 26.0 %all-to-all-start.4 = ((bf16[192,8,512]{2,0,1:T(8,128)(2,1)}), bf16[192,8,512]{2,0,1:T(8,128)(2,1)S(1)}, u32[]{:S(2)}, u32[]{:S(2)}) async-start(bf16[192,8,512]{2,0,1:T(8,128)(2,1)} %copy.20), calls=%async_computation.4 | async-start | bytes 3145728 | tf_op jit(solution)/shard_map/all_to_all | solution.py:98
  380.7 4.3 copy-start.2
  387.7 15.4 %copy-start.3 = (bf16[192,224]{1,0:T(8,128)(2,1)}, bf16[192,224]{1,0:T(8,128)(2,1)S(1)}, u32[]{:S(2)}) copy-start(bf16[192,224]{1,0:T(8,128)(2,1)S(1)} %get-tuple-element.12) | copy-start | bytes 258052
  403.2 16.6 %all-to-all-start.5 = ((bf16[8,192,224]{2,1,0:T(8,128)(2,1)}), bf16[8,192,224]{2,1,0:T(8,128)(2,1)S(1)}, u32[]{:S(2)}, u32[]{:S(2)}) async-start(bf16[8,192,224]{2,1,0:T(8,128)(2,1)} %stack.2), calls=%async_computation.5 | async-start | bytes 1572864 | tf_op jit(solution)/shard_map/all_to_all | solution.py:103
  406.7 2.3 copy-start.1
  419.8 106.4 %all-to-all-start.3 = ((bf16[64,3,4096]{2,1,0:T(4,128)(2,1)}), bf16[64,3,4096]{2,1,0:T(4,128)(2,1)}, u32[]{:S(2)}, u32[]{:S(2)}) async-start(bf16[64,3,4096]{2,1,0:T(4,128)(2,1)} %all_to_all.45), calls=%async_computation.3 | async-start | bytes 4194304 | tf_op jit(solution)/shard_map/all_to_all | solution.py:95
Sparse Core Ops, SparseCore 0:
  10.1 36.9 all-gather.5
  49.2 32.9 all-gather.3
  84.3 32.8 all-gather.7
